TPU v7x, 512 devices: a whole 4x8x8 slice. The times are simulated.
512 devices in a mesh: region: 8 (over x, core), owner: 64 (over y, z).
Axes of the slice: x: 4, y: 8, z: 8, core: 2. Of those that a mesh axis runs over, the one named last changes fastest.
Arguments:
- voxels: bfloat16 [8, 64, 1, 256, 1024], P('region', 'owner'), may hold values from -6 to 6
- norm_gain: float32 [1024], replicated, may hold values from 0.5 to 1.5
- qkv_weight: bfloat16 [1024, 3072], P(('region', 'owner')), may hold values from -0.14453125 to 0.14453125
- out_weight: bfloat16 [1024, 1024], P(('region', 'owner')), may hold values from -0.1875 to 0.1875
- neighbours: int32 [8, 64, 1, 8], P('region', 'owner'), may hold values from -1 to 511, as said below
Outputs:
- attended_voxels: bfloat16 [8, 64, 1, 256, 1024], P('region', 'owner')
Inputs may be any that keep to these rules, and one draw needn't show every extreme that they name: `neighbours`: each entry is -1 or the number (r * 64 + o) + c of a block c held by the device at region r and owner o, where r and o each differ by at most one from those of the list's own block; a list never names its own block and names no block twice.
All inputs are finite; a program needn't handle non-finite values.
Results may differ from a plain program's by a relative error of at most 0.0057.
Values may be sent and summed in bfloat16 or wider, within the bound.
No kernel may reach another device: no remote copies, remote signals or barrier semaphores. Data moves between devices by JAX's collectives and lax.ppermute only.
A program may use at most 64 MiB of HBM per device.

v0:
```python
import jax
import jax.numpy as jnp
from jax import lax
from jax.sharding import PartitionSpec as P

HEAD_DIM = 64


def in_order(blocks, dim):
    shape = list(blocks.shape[1:])
    shape[dim] *= blocks.shape[0]
    return jnp.moveaxis(blocks, 0, dim).reshape(shape)


def from_everyone(value, axis):
    devices = lax.axis_size(axis)
    return lax.all_to_all(
        jnp.broadcast_to(value[None], (devices, *value.shape)), axis, 0, 0, tiled=True
    )


def gathered_copies(value, axis, dim):
    return in_order(from_everyone(value, axis), dim)


def padded(value, sides, width):
    for axis, dim in sides:
        devices, length = (lax.axis_size(axis), value.shape[dim])
        up = [(i, (i + 1) % devices) for i in range(devices - 1)]
        down = [(j, i) for i, j in up]
        last = lax.slice_in_dim(value, length - width, length, axis=dim)
        first = lax.slice_in_dim(value, 0, width, axis=dim)
        before = lax.ppermute(last, axis, up)
        after = lax.ppermute(first, axis, down)
        value = jnp.concatenate([before, value, after], axis=dim)
    return value


def layer_norm(inputs, norm_gain):
    widened = inputs.astype(jnp.float32)
    average = jnp.mean(widened, axis=-1, keepdims=True)
    spread = jnp.mean((widened - average) ** 2, axis=-1, keepdims=True)
    return ((widened - average) * lax.rsqrt(spread + 1e-06) * norm_gain).astype(jnp.bfloat16)


def shards(voxels, norm_gain, qkv_weight, out_weight, neighbours):
    capacity = voxels.shape[2]
    block_size = voxels.shape[3]
    model_width = voxels.shape[4]
    token_count = capacity * block_size
    flat_tokens = voxels.reshape(token_count, model_width)
    normed = layer_norm(flat_tokens, norm_gain)
    group_rows = gathered_copies(qkv_weight, "owner", 0)
    columns = normed
    qkv = jnp.dot(
        columns,
        lax.all_gather(group_rows, "region", axis=0, tiled=True),
        preferred_element_type=jnp.float32,
    )
    qkv = qkv.astype(jnp.bfloat16)
    queries = qkv[:, :model_width].reshape(capacity, block_size, model_width)
    kv_pairs = qkv[:, model_width:].reshape(1, 1, capacity, block_size, 2 * model_width)
    extended = padded(kv_pairs, (("region", 0), ("owner", 1)), 1)
    extended = extended.reshape(9 * capacity * block_size, 2 * model_width)
    key_rows = extended[:, :model_width]
    value_rows = extended[:, model_width:]
    owner_count = lax.axis_size("owner")
    my_region = lax.axis_index("region")
    my_owner = lax.axis_index("owner")
    list_ids = neighbours.reshape(capacity, neighbours.shape[-1])
    far_region = list_ids // (owner_count * capacity)
    far_owner = list_ids // capacity % owner_count
    far_slot = list_ids % capacity
    local_ids = (
        (far_region - my_region + 1) * 3 + (far_owner - my_owner + 1)
    ) * capacity + far_slot
    local_ids = jnp.where(list_ids >= 0, local_ids, -1)
    slot_ids = jnp.arange(9 * capacity, dtype=jnp.int32)
    listed = jnp.any(local_ids[:, :, None] == slot_ids[None, None, :], axis=1)
    own_block = slot_ids[None, :] == (4 * capacity + jnp.arange(capacity, dtype=jnp.int32))[:, None]
    allowed = listed | own_block
    key_mask = jnp.repeat(allowed, block_size, axis=1)
    group_heads = 2
    group_cols = group_heads * HEAD_DIM
    group_count = model_width // group_cols
    score_scale = HEAD_DIM ** (-0.5)

    def attend_group(group_idx, buffer):
        offset = group_idx * group_cols
        query_part = lax.dynamic_slice_in_dim(queries, offset, group_cols, 2).reshape(
            capacity, block_size, group_heads, HEAD_DIM
        )
        key_part = lax.dynamic_slice_in_dim(key_rows, offset, group_cols, 1).reshape(
            -1, group_heads, HEAD_DIM
        )
        value_part = lax.dynamic_slice_in_dim(value_rows, offset, group_cols, 1).reshape(
            -1, group_heads, HEAD_DIM
        )
        scores = (
            jnp.einsum("cshd,khd->chsk", query_part, key_part, preferred_element_type=jnp.float32)
            * score_scale
        )
        scores = jnp.where(key_mask[:, None, None, :], scores, -1e30)
        row_max = jnp.max(scores, axis=-1, keepdims=True)
        shifted = jnp.exp(scores - row_max)
        attn_probs = (shifted / jnp.sum(shifted, axis=-1, keepdims=True)).astype(jnp.bfloat16)
        attended = jnp.einsum(
            "chsk,khd->cshd", attn_probs, value_part, preferred_element_type=jnp.float32
        )
        attended = attended.astype(jnp.bfloat16).reshape(capacity, block_size, group_cols)
        return lax.dynamic_update_slice_in_dim(buffer, attended, offset, 2)

    mixed = lax.fori_loop(
        0, group_count, attend_group, jnp.zeros((capacity, block_size, model_width), jnp.bfloat16)
    )
    mixed_rows = mixed.reshape(token_count, model_width)
    columns = mixed_rows
    projected = jnp.dot(
        columns,
        lax.all_gather(out_weight, ("region", "owner"), axis=0, tiled=True),
        preferred_element_type=jnp.float32,
    )
    result = flat_tokens.astype(jnp.float32) + projected
    return result.astype(jnp.bfloat16).reshape(voxels.shape)


def solution(mesh):
    return jax.shard_map(
        shards,
        mesh=mesh,
        in_specs=(
            P("region", "owner", None, None, None),
            P(),
            P(("region", "owner"), None),
            P(("region", "owner"), None),
            P("region", "owner", None, None),
        ),
        out_specs=P("region", "owner", None, None, None),
        check_vma=False,
    )
```

profile of v0, /device:TPU:1, one launch (start us, length us, event | category | flops | bytes accessed | tf_op | source)
XLA Modules:
  0.0 356.1 jit_solution(15957770580684786674)
XLA Ops:
  8.5 38.6 %all_to_all.5 = bf16[64,2,3072]{2,1,0:T(2,128)(2,1)S(1)} all-to-all(bf16[64,2,3072]{2,1,0:T(2,128)(2,1)S(1)} %broadcast_in_dim.53), channel_id=1, replica_groups=mesh['region'=8,'owner'=64] {'owner'}, dimensions={0} | all-to-all | bytes 1572864 | tf_op jit(solution)/shard_map/all_to_all | solution.py:17
  48.9 43.2 %all-gather.4.cloned.1.call-done = bf16[1024,3072]{1,0:T(8,128)(2,1)} async-done(((bf16[128,3072]{1,0:T(8,128)(2,1)}), bf16[1024,3072]{1,0:T(8,128)(2,1)}) %all-gather.4.cloned.1.call-update) | async-done | bytes 6291472 | tf_op jit(solution)/shard_map/all_gather | solution.py:57
  92.1 4.7 %convolution_convert_fusion = bf16[256,3072]{1,0:T(8,128)(2,1)S(1)} fusion(bf16[1024,3072]{1,0:T(8,128)(2,1)} %all-gather.4.cloned.1.call-done, bf16[1,1,1,256,1024]{4,3,2,1,0:T(8,128)(2,1)S(1)} %copy-done.2, f32[1024]{0:T(1024)S(1)} %copy-done.8, f32[256]{0:T(256)S(1)} %add_rsqrt_fusion, f32[256]{0:T(256)S(1)} %broadcast_multiply_fusion), kind=kOutput, calls=%fused_computation.17 | convolution fusion | flops 1612709888 | bytes 8394752 | tf_op jit(solution)/shard_map/dot_general | solution.py:55
  98.0 2.4 collective-permute-start
  100.4 2.0 collective-permute-start.1
  102.4 9.7 %collective-permute-done = bf16[1,1,1,256,2048]{4,3,2,1,0:T(8,128)(2,1)S(1)} collective-permute-done((bf16[1,1,1,256,2048]{4,3,2,1,0:T(8,128)(2,1)S(1)}, bf16[1,1,1,256,2048]{4,3,2,1,0:T(8,128)(2,1)S(1)}, u32[]{:S(2)}, u32[]{:S(2)}) %collective-permute-start) | collective-permute-done | bytes 1048608 | tf_op jit(solution)/shard_map/ppermute | solution.py:33
  112.1 4.4 %collective-permute-done.1 = bf16[1,1,1,256,2048]{4,3,2,1,0:T(8,128)(2,1)S(1)} collective-permute-done((bf16[1,1,1,256,2048]{4,3,2,1,0:T(8,128)(2,1)S(1)}, bf16[1,1,1,256,2048]{4,3,2,1,0:T(8,128)(2,1)S(1)}, u32[]{:S(2)}, u32[]{:S(2)}) %collective-permute-start.1) | collective-permute-done | bytes 1048608 | tf_op jit(solution)/shard_map/ppermute | solution.py:34
  116.5 2.1 pad_maximum_fusion.1
  118.5 5.4 %collective-permute-start.2 = (bf16[3,1,1,256,2048]{4,3,2,1,0:T(8,128)(2,1)}, bf16[3,1,1,256,2048]{4,3,2,1,0:T(8,128)(2,1)}, u32[]{:S(2)}, u32[]{:S(2)}) collective-permute-start(bf16[3,1,1,256,2048]{4,3,2,1,0:T(8,128)(2,1)} %pad_maximum_fusion.1), channel_id=1, source_target_pairs={{0,1},{1,2},{2,3},{3,4},{4,5},{5,6},{6,7},{7,8},{8,9},{9,10},{10,1... | collective-permute-start | bytes 9437192 | tf_op jit(solution)/shard_map/ppermute | solution.py:33
  125.3 118.2 %all-gather.6.cloned.1.call-done = bf16[512,2,1024]{2,1,0:T(2,128)(2,1)} async-done(((bf16[1,2,1024]{2,1,0:T(2,128)(2,1)}), bf16[512,2,1024]{2,1,0:T(2,128)(2,1)}) %all-gather.6.cloned.1.call-update) | async-done | bytes 2097168 | tf_op jit(solution)/shard_map/all_gather | solution.py:120
  243.5 4.1 %reshape.300 = bf16[1024,1024]{1,0:T(8,128)(2,1)} reshape(bf16[512,2,1024]{2,1,0:T(2,128)(2,1)} %all-gather.6.cloned.1.call-done) | data formatting | bytes 4194304
  247.6 1.9 slice_bitcast_fusion.1
  249.5 4.7 %pad_maximum_fusion = bf16[3,3,1,256,2048]{4,3,2,1,0:T(8,128)(2,1)S(1)} fusion(bf16[3,1,1,256,2048]{4,3,2,1,0:T(8,128)(2,1)} %collective-permute-done.3, bf16[1,1,1,256,2048]{4,3,2,1,0:T(8,128)(2,1)} %copy-done.5, bf16[1,1,1,256,2048]{4,3,2,1,0:T(8,128)(2,1)} %copy-done.1, bf16[1,1,1,256,2048]{4,3,2,1,0:T(8,128)(2,1)} %copy-done.4, ...), kind=kLoop, calls=%fused_computation.16 | loop fusion | flops 18874368 | bytes 18874368 | tf_op jit(solution)/shard_map/concatenate | solution.py:35
  254.2 4.8 %fusion.28 = (bf16[2304,1024]{1,0:T(8,128)(2,1)}, bf16[2304,1024]{1,0:T(8,128)(2,1)}) fusion(bf16[2304,2048]{1,0:T(8,128)(2,1)S(1)} %bitcast.105), kind=kLoop, calls=%fused_computation.51 | loop fusion | bytes 18874368 | tf_op jit(solution)/shard_map/slice | solution.py:65
  259.0 86.5 %while.14 = (s32[]{:T(128)}, bf16[1,256,1024]{1,2,0:T(8,128)(2,1)S(1)}, bf16[2304,1024]{1,0:T(8,128)(2,1)}, bf16[2304,1024]{1,0:T(8,128)(2,1)}, bf16[1,256,1024]...) while((s32[]{:T(128)}, ...), condition=%wide.region_6.7_spmd.clone, body=%wide.region_3.6_spmd.clone.sunk | while | flops 311458816 | bytes 39472324 | solution.py:113
  263.5 2.2 copy-done
  266.6 3.3 fusion.45
  274.3 2.2 copy-done
  277.4 3.3 fusion.45
  285.1 2.2 copy-done
  288.2 3.3 fusion.45
  295.9 2.2 copy-done
  299.0 3.3 fusion.45
  306.7 2.2 copy-done
  309.8 3.3 fusion.45
  317.5 2.2 copy-done
  320.6 3.3 fusion.45
  328.3 2.2 copy-done
  331.4 3.3 fusion.45
  339.1 2.2 copy-done
  342.2 3.3 fusion.45
  345.5 3.1 fusion.15
  (122 shorter events, 47.7 us)
Async XLA Ops:
  7.4 41.1 %copy-start.2 = (bf16[1,1,1,256,1024]{4,3,2,1,0:T(8,128)(2,1)S(1)}, bf16[1,1,1,256,1024]{4,3,2,1,0:T(8,128)(2,1)}, u32[]{:S(2)}) copy-start(bf16[1,1,1,256,1024]{4,3,2,1,0:T(8,128)(2,1)} %param.7) | copy-start | bytes 1572868
  7.4 84.7 %copy-start.8 = (f32[1024]{0:T(1024)S(1)}, f32[1024]{0:T(1024)}, u32[]{:S(2)}) copy-start(f32[1024]{0:T(1024)} %param.8) | copy-start | bytes 12292
  7.4 84.7 %all-gather.4.cloned.1.call-start = ((), (), s32[]{:S(2)}) async-start(), calls=%async_computation.1 | async-start | bytes 7077888 | tf_op jit(solution)/shard_map/all_gather | solution.py:57
  48.4 195.1 %all-gather.6.cloned.1.call-start = ((), (), s32[]{:S(2)}) async-start(), calls=%async_computation.2 | async-start | bytes 2101248 | tf_op jit(solution)/shard_map/all_gather | solution.py:120
  96.8 1.2 copy-start.6
  96.8 28.4 %copy-start.7 = (s32[1,1,1,8]{3,2,1,0:T(1,128)S(1)}, s32[1,1,1,8]{3,2,1,0:T(1,128)}, u32[]{:S(2)}) copy-start(s32[1,1,1,8]{3,2,1,0:T(1,128)} %param.11) | copy-start | bytes 100
  98.0 149.6 %copy-start.1 = (bf16[1,1,1,256,2048]{4,3,2,1,0:T(8,128)(2,1)}, bf16[1,1,1,256,2048]{4,3,2,1,0:T(8,128)(2,1)S(1)}, u32[]{:S(2)}) copy-start(bf16[1,1,1,256,2048]{4,3,2,1,0:T(8,128)(2,1)S(1)} %slice_bitcast_fusion) | copy-start | bytes 3145732
  98.0 14.1 %collective-permute-start = (bf16[1,1,1,256,2048]{4,3,2,1,0:T(8,128)(2,1)S(1)}, bf16[1,1,1,256,2048]{4,3,2,1,0:T(8,128)(2,1)S(1)}, u32[]{:S(2)}, u32[]{:S(2)}) collective-permute-start(bf16[1,1,1,256,2048]{4,3,2,1,0:T(8,128)(2,1)S(1)} %slice_bitcast_fusion), channel_id=1, source_target_pairs={{0,64},{64,128},{128,192},{192,256},{256,320},{320,384},{384,448},... | collective-permute-start | bytes 3145736 | tf_op jit(solution)/shard_map/ppermute | solution.py:33
  100.4 16.1 %collective-permute-start.1 = (bf16[1,1,1,256,2048]{4,3,2,1,0:T(8,128)(2,1)S(1)}, bf16[1,1,1,256,2048]{4,3,2,1,0:T(8,128)(2,1)S(1)}, u32[]{:S(2)}, u32[]{:S(2)}) collective-permute-start(bf16[1,1,1,256,2048]{4,3,2,1,0:T(8,128)(2,1)S(1)} %slice_bitcast_fusion), channel_id=1, source_target_pairs={{64,0},{128,64},{192,128},{256,192},{320,256},{384,320},{448,384},... | collective-permute-start | bytes 3145736 | tf_op jit(solution)/shard_map/ppermute | solution.py:34
  112.1 135.5 %copy-start.4 = (bf16[1,1,1,256,2048]{4,3,2,1,0:T(8,128)(2,1)}, bf16[1,1,1,256,2048]{4,3,2,1,0:T(8,128)(2,1)S(1)}, u32[]{:S(2)}) copy-start(bf16[1,1,1,256,2048]{4,3,2,1,0:T(8,128)(2,1)S(1)} %collective-permute-done) | copy-start | bytes 3145732
  116.5 131.1 %copy-start.5 = (bf16[1,1,1,256,2048]{4,3,2,1,0:T(8,128)(2,1)}, bf16[1,1,1,256,2048]{4,3,2,1,0:T(8,128)(2,1)S(1)}, u32[]{:S(2)}) copy-start(bf16[1,1,1,256,2048]{4,3,2,1,0:T(8,128)(2,1)S(1)} %collective-permute-done.1) | copy-start | bytes 3145732
  118.5 130.9 %collective-permute-start.2 = (bf16[3,1,1,256,2048]{4,3,2,1,0:T(8,128)(2,1)}, bf16[3,1,1,256,2048]{4,3,2,1,0:T(8,128)(2,1)}, u32[]{:S(2)}, u32[]{:S(2)}) collective-permute-start(bf16[3,1,1,256,2048]{4,3,2,1,0:T(8,128)(2,1)} %pad_maximum_fusion.1), channel_id=1, source_target_pairs={{0,1},{1,2},{2,3},{3,4},{4,5},{5,6},{6,7},{7,8},{8,9},{9,10},{10,1... | collective-permute-start | bytes 9437192 | tf_op jit(solution)/shard_map/ppermute | solution.py:33
  123.9 125.6 %collective-permute-start.3 = (bf16[3,1,1,256,2048]{4,3,2,1,0:T(8,128)(2,1)}, bf16[3,1,1,256,2048]{4,3,2,1,0:T(8,128)(2,1)}, u32[]{:S(2)}, u32[]{:S(2)}) collective-permute-start(bf16[3,1,1,256,2048]{4,3,2,1,0:T(8,128)(2,1)} %pad_maximum_fusion.1), channel_id=1, source_target_pairs={{1,0},{2,1},{3,2},{4,3},{5,4},{6,5},{7,6},{8,7},{9,8},{10,9},{11,1... | collective-permute-start | bytes 9437192 | tf_op jit(solution)/shard_map/ppermute | solution.py:34
  259.0 86.5 %copy-start.3 = (bf16[1,1,1,256,1024]{4,3,2,1,0:T(8,128)(2,1)S(1)}, bf16[1,1,1,256,1024]{4,3,2,1,0:T(8,128)(2,1)}, u32[]{:S(2)}) copy-start(bf16[1,1,1,256,1024]{4,3,2,1,0:T(8,128)(2,1)} %param.7) | copy-start | bytes 1572868
  263.4 2.2 copy-start
  274.3 2.2 copy-start
  285.1 2.2 copy-start
  295.9 2.2 copy-start
  306.7 2.2 copy-start
  317.5 2.2 copy-start
  328.3 2.2 copy-start
  339.1 2.2 copy-start
Sparse Core Ops, SparseCore 0:
  48.5 43.5 all-gather.3
Sparse Core Ops, SparseCore 1:
  102.5 140.9 all-gather.5
where the time goes:
time: 357 us; the launch traced here: 356 us
  waiting for transfers between devices  175 us (49%)
  local copies, waits for them, and re-layouts  55.3 us (15%)
  matrix products  47.8 us (13%)
  blocking collectives  38.6 us (11%)
  between operations  15 us (4%)
  other arithmetic  12.3 us (3%)
  starting transfers between devices  11.1 us (3%)
    all_gather x1, waiting for transfers between devices, shards(): lax.all_gather(out_weight, ('region', 'owner'), axis=0, tiled=True)  118 us
    all_gather x1, waiting for transfers between devices, shards(): lax.all_gather(group_rows, 'region', axis=0, tiled=True)  43.2 us
    all_to_all x1, blocking collectives, from_everyone(): lax.all_to_all(jnp.broadcast_to(value[None], (devices, *value.shape)), ax...  38.6 us
    dot_general x8, matrix products, attend_group(): jnp.einsum('chsk,khd->cshd', attn_probs, value_part, preferred_element_ty...  26.1 us
    while x16, local copies, waits for them, and re-layouts  17.8 us
    dot_general x8, matrix products, attend_group(): jnp.einsum('cshd,khd->chsk', query_part, key_part, preferred_element_type...  13.9 us
    dynamic_slice x16, local copies, waits for them, and re-layouts, attend_group(): lax.dynamic_slice_in_dim(key_rows, offset, group_cols, 1)  12.8 us
    ppermute x2, waiting for transfers between devices, padded(): before = lax.ppermute(last, axis, up)  9.66 us
  transfers between devices with their start and end apart: 6, of which 4 were waited for; matrix products, arithmetic and copies ran while one was open for 2% of the time, Pallas kernels for 0%

commit v1 on v0

--- a/solution.py
+++ b/solution.py
@@ -4,6 +4,11 @@
 from jax.sharding import PartitionSpec as P
 
 HEAD_DIM = 64
+
+
+def exchange_gather(block, name, along):
+    sent = jnp.stack([block] * lax.axis_size(name))
+    return jnp.concatenate(lax.all_to_all(sent, name, 0, 0), axis=along)
 
 
 def in_order(blocks, dim):
@@ -53,9 +58,7 @@
     group_rows = gathered_copies(qkv_weight, "owner", 0)
     columns = normed
     qkv = jnp.dot(
-        columns,
-        lax.all_gather(group_rows, "region", axis=0, tiled=True),
-        preferred_element_type=jnp.float32,
+        columns, exchange_gather(group_rows, "region", 0), preferred_element_type=jnp.float32
     )
     qkv = qkv.astype(jnp.bfloat16)
     queries = qkv[:, :model_width].reshape(capacity, block_size, model_width)

time: 357 us -> 392 us (1.098)
  waiting for transfers between devices: 175 us -> 201 us
  starting transfers between devices: 11.1 us -> 18.7 us
    all_to_all x0 -> x1, waiting for transfers between devices: none -> 70.8 us  [exchange_gather(): return jnp.concatenate(lax.all_to_all(sent, name, 0, 0), axis=along)]
    all_gather x1 -> x0, waiting for transfers between devices: 43.2 us -> none  [shards(): lax.all_gather(group_rows, 'region', axis=0, tiled=True)]
    all_to_all x0 -> x1, starting transfers between devices: none -> 7.55 us  [exchange_gather(): return jnp.concatenate(lax.all_to_all(sent, name, 0, 0), axis=along)]
where the time goes in v1:
time: 392 us; the launch traced here: 390 us
  waiting for transfers between devices  201 us (51%)
  local copies, waits for them, and re-layouts  57.8 us (15%)
  matrix products  47.8 us (12%)
  blocking collectives  38.6 us (10%)
  starting transfers between devices  18.7 us (5%)
  between operations  13.5 us (3%)
  other arithmetic  12.3 us (3%)
    all_gather x1, waiting for transfers between devices, shards(): lax.all_gather(out_weight, ('region', 'owner'), axis=0, tiled=True)  116 us
    all_to_all x1, waiting for transfers between devices, exchange_gather(): return jnp.concatenate(lax.all_to_all(sent, name, 0, 0), axis=along)  70.8 us
    all_to_all x1, blocking collectives, from_everyone(): lax.all_to_all(jnp.broadcast_to(value[None], (devices, *value.shape)), ax...  38.6 us
    dot_general x8, matrix products, attend_group(): jnp.einsum('chsk,khd->cshd', attn_probs, value_part, preferred_element_ty...  26.1 us
    while x16, local copies, waits for them, and re-layouts  17.8 us
    dot_general x8, matrix products, attend_group(): jnp.einsum('cshd,khd->chsk', query_part, key_part, preferred_element_type...  13.9 us
    dynamic_slice x16, local copies, waits for them, and re-layouts, attend_group(): lax.dynamic_slice_in_dim(key_rows, offset, group_cols, 1)  12.8 us
    ppermute x2, waiting for transfers between devices, padded(): before = lax.ppermute(last, axis, up)  9.77 us
  transfers between devices with their start and end apart: 6, of which 4 were waited for; matrix products, arithmetic and copies ran while one was open for 2% of the time, Pallas kernels for 0%

profile of v1, /device:TPU:1, one launch (start us, length us, event | category | flops | bytes accessed | tf_op | source)
XLA Modules:
  0.0 390.5 jit_solution(2913370229700516287)
XLA Ops:
  7.7 38.6 %all_to_all.10 = bf16[64,2,3072]{2,1,0:T(2,128)(2,1)S(1)} all-to-all(bf16[64,2,3072]{2,1,0:T(2,128)(2,1)S(1)} %broadcast_in_dim.53), channel_id=1, replica_groups=mesh['region'=8,'owner'=64] {'owner'}, dimensions={0} | all-to-all | bytes 1572864 | tf_op jit(solution)/shard_map/all_to_all | solution.py:22
  46.6 3.4 stack.3
  50.0 7.6 %all-to-all-start.1 = ((bf16[8,128,3072]{2,1,0:T(8,128)(2,1)}), bf16[8,128,3072]{2,1,0:T(8,128)(2,1)}, u32[]{:S(2)}, u32[]{:S(2)}) async-start(bf16[8,128,3072]{2,1,0:T(8,128)(2,1)} %stack.3), calls=%async_computation.1 | async-start | bytes 12582912 | tf_op jit(solution)/shard_map/all_to_all | solution.py:11
  58.0 70.8 %all-to-all-done.1 = bf16[8,128,3072]{2,1,0:T(8,128)(2,1)} async-done(((bf16[8,128,3072]{2,1,0:T(8,128)(2,1)}), bf16[8,128,3072]{2,1,0:T(8,128)(2,1)}, u32[]{:S(2)}, u32[]{:S(2)}) %all-to-all-start.1) | async-done | bytes 6291488 | tf_op jit(solution)/shard_map/all_to_all | solution.py:11
  128.9 4.7 %convolution_convert_fusion = bf16[256,3072]{1,0:T(8,128)(2,1)S(1)} fusion(bf16[1024,3072]{1,0:T(8,128)(2,1)} %bitcast.2, bf16[1,1,1,256,1024]{4,3,2,1,0:T(8,128)(2,1)S(1)} %copy-done.2, f32[1024]{0:T(1024)S(1)} %copy-done.8, f32[256]{0:T(256)S(1)} %add_rsqrt_fusion, f32[256]{0:T(256)S(1)} %broadcast_multiply_fusion), kind=kOutput, calls=%fused_computation.17 | convolution fusion | flops 1612709888 | bytes 8394752 | tf_op jit(solution)/shard_map/dot_general | solution.py:60
  134.7 3.0 collective-permute-start
  139.7 9.8 %collective-permute-done = bf16[1,1,1,256,2048]{4,3,2,1,0:T(8,128)(2,1)S(1)} collective-permute-done((bf16[1,1,1,256,2048]{4,3,2,1,0:T(8,128)(2,1)S(1)}, bf16[1,1,1,256,2048]{4,3,2,1,0:T(8,128)(2,1)S(1)}, u32[]{:S(2)}, u32[]{:S(2)}) %collective-permute-start) | collective-permute-done | bytes 1048608 | tf_op jit(solution)/shard_map/ppermute | solution.py:38
  149.5 4.8 %collective-permute-done.1 = bf16[1,1,1,256,2048]{4,3,2,1,0:T(8,128)(2,1)S(1)} collective-permute-done((bf16[1,1,1,256,2048]{4,3,2,1,0:T(8,128)(2,1)S(1)}, bf16[1,1,1,256,2048]{4,3,2,1,0:T(8,128)(2,1)S(1)}, u32[]{:S(2)}, u32[]{:S(2)}) %collective-permute-start.1) | collective-permute-done | bytes 1048608 | tf_op jit(solution)/shard_map/ppermute | solution.py:39
  154.3 2.0 pad_maximum_fusion.1
  156.4 4.9 %collective-permute-start.2 = (bf16[3,1,1,256,2048]{4,3,2,1,0:T(8,128)(2,1)}, bf16[3,1,1,256,2048]{4,3,2,1,0:T(8,128)(2,1)}, u32[]{:S(2)}, u32[]{:S(2)}) collective-permute-start(bf16[3,1,1,256,2048]{4,3,2,1,0:T(8,128)(2,1)} %pad_maximum_fusion.1), channel_id=1, source_target_pairs={{0,1},{1,2},{2,3},{3,4},{4,5},{5,6},{6,7},{7,8},{8,9},{9,10},{10,1... | collective-permute-start | bytes 9437192 | tf_op jit(solution)/shard_map/ppermute | solution.py:38
  162.7 115.7 %all-gather.3.cloned.1.call-done = bf16[512,2,1024]{2,1,0:T(2,128)(2,1)} async-done(((bf16[1,2,1024]{2,1,0:T(2,128)(2,1)}), bf16[512,2,1024]{2,1,0:T(2,128)(2,1)}) %all-gather.3.cloned.1.call-update) | async-done | bytes 2097168 | tf_op jit(solution)/shard_map/all_gather | solution.py:123
  278.5 4.1 %reshape.323 = bf16[1024,1024]{1,0:T(8,128)(2,1)} reshape(bf16[512,2,1024]{2,1,0:T(2,128)(2,1)} %all-gather.3.cloned.1.call-done) | data formatting | bytes 4194304
  284.4 4.7 %pad_maximum_fusion = bf16[3,3,1,256,2048]{4,3,2,1,0:T(8,128)(2,1)S(1)} fusion(bf16[3,1,1,256,2048]{4,3,2,1,0:T(8,128)(2,1)} %collective-permute-done.3, bf16[1,1,1,256,2048]{4,3,2,1,0:T(8,128)(2,1)} %copy-done.5, bf16[1,1,1,256,2048]{4,3,2,1,0:T(8,128)(2,1)} %copy-done.1, bf16[1,1,1,256,2048]{4,3,2,1,0:T(8,128)(2,1)} %copy-done.4, ...), kind=kLoop, calls=%fused_computation.16 | loop fusion | flops 18874368 | bytes 18874368 | tf_op jit(solution)/shard_map/concatenate | solution.py:40
  289.1 4.8 %fusion.29 = (bf16[2304,1024]{1,0:T(8,128)(2,1)}, bf16[2304,1024]{1,0:T(8,128)(2,1)}) fusion(bf16[2304,2048]{1,0:T(8,128)(2,1)S(1)} %bitcast.102), kind=kLoop, calls=%fused_computation.53 | loop fusion | bytes 18874368 | tf_op jit(solution)/shard_map/slice | solution.py:68
  293.9 86.6 %while.14 = (s32[]{:T(128)}, bf16[1,256,1024]{1,2,0:T(8,128)(2,1)S(1)}, bf16[2304,1024]{1,0:T(8,128)(2,1)}, bf16[2304,1024]{1,0:T(8,128)(2,1)}, bf16[1,256,1024]...) while((s32[]{:T(128)}, ...), condition=%wide.region_6.7_spmd.clone, body=%wide.region_3.6_spmd.clone.sunk | while | flops 311458816 | bytes 39472324 | solution.py:116
  298.4 2.2 copy-done
  301.5 3.3 fusion.46
  309.2 2.2 copy-done
  312.3 3.3 fusion.46
  320.0 2.2 copy-done
  323.1 3.3 fusion.46
  330.8 2.2 copy-done
  333.9 3.3 fusion.46
  341.6 2.2 copy-done
  344.7 3.3 fusion.46
  352.5 2.2 copy-done
  355.6 3.3 fusion.46
  363.3 2.2 copy-done
  366.4 3.3 fusion.46
  374.1 2.2 copy-done
  377.2 3.3 fusion.46
  380.5 3.1 fusion.13
  (122 shorter events, 50.5 us)
Async XLA Ops:
  50.0 7.6 %copy-start.2 = (bf16[1,1,1,256,1024]{4,3,2,1,0:T(8,128)(2,1)S(1)}, bf16[1,1,1,256,1024]{4,3,2,1,0:T(8,128)(2,1)}, u32[]{:S(2)}) copy-start(bf16[1,1,1,256,1024]{4,3,2,1,0:T(8,128)(2,1)} %param.7) | copy-start | bytes 1572868
  50.0 78.8 %copy-start.8 = (f32[1024]{0:T(1024)S(1)}, f32[1024]{0:T(1024)}, u32[]{:S(2)}) copy-start(f32[1024]{0:T(1024)} %param.8) | copy-start | bytes 12292
  50.0 78.8 %all-to-all-start.1 = ((bf16[8,128,3072]{2,1,0:T(8,128)(2,1)}), bf16[8,128,3072]{2,1,0:T(8,128)(2,1)}, u32[]{:S(2)}, u32[]{:S(2)}) async-start(bf16[8,128,3072]{2,1,0:T(8,128)(2,1)} %stack.3), calls=%async_computation.1 | async-start | bytes 12582912 | tf_op jit(solution)/shard_map/all_to_all | solution.py:11
  57.6 220.9 %all-gather.3.cloned.1.call-start = ((), (), s32[]{:S(2)}) async-start(), calls=%async_computation.2 | async-start | bytes 2101248 | tf_op jit(solution)/shard_map/all_gather | solution.py:123
  133.5 1.2 copy-start.6
  133.6 29.0 %copy-start.7 = (s32[1,1,1,8]{3,2,1,0:T(1,128)S(1)}, s32[1,1,1,8]{3,2,1,0:T(1,128)}, u32[]{:S(2)}) copy-start(s32[1,1,1,8]{3,2,1,0:T(1,128)} %param.11) | copy-start | bytes 100
  134.7 147.8 %copy-start.1 = (bf16[1,1,1,256,2048]{4,3,2,1,0:T(8,128)(2,1)}, bf16[1,1,1,256,2048]{4,3,2,1,0:T(8,128)(2,1)S(1)}, u32[]{:S(2)}) copy-start(bf16[1,1,1,256,2048]{4,3,2,1,0:T(8,128)(2,1)S(1)} %slice_bitcast_fusion) | copy-start | bytes 3145732
  134.7 14.8 %collective-permute-start = (bf16[1,1,1,256,2048]{4,3,2,1,0:T(8,128)(2,1)S(1)}, bf16[1,1,1,256,2048]{4,3,2,1,0:T(8,128)(2,1)S(1)}, u32[]{:S(2)}, u32[]{:S(2)}) collective-permute-start(bf16[1,1,1,256,2048]{4,3,2,1,0:T(8,128)(2,1)S(1)} %slice_bitcast_fusion), channel_id=1, source_target_pairs={{0,64},{64,128},{128,192},{192,256},{256,320},{320,384},{384,448},... | collective-permute-start | bytes 3145736 | tf_op jit(solution)/shard_map/ppermute | solution.py:38
  137.8 16.5 %collective-permute-start.1 = (bf16[1,1,1,256,2048]{4,3,2,1,0:T(8,128)(2,1)S(1)}, bf16[1,1,1,256,2048]{4,3,2,1,0:T(8,128)(2,1)S(1)}, u32[]{:S(2)}, u32[]{:S(2)}) collective-permute-start(bf16[1,1,1,256,2048]{4,3,2,1,0:T(8,128)(2,1)S(1)} %slice_bitcast_fusion), channel_id=1, source_target_pairs={{64,0},{128,64},{192,128},{256,192},{320,256},{384,320},{448,384},... | collective-permute-start | bytes 3145736 | tf_op jit(solution)/shard_map/ppermute | solution.py:39
  149.5 133.0 %copy-start.4 = (bf16[1,1,1,256,2048]{4,3,2,1,0:T(8,128)(2,1)}, bf16[1,1,1,256,2048]{4,3,2,1,0:T(8,128)(2,1)S(1)}, u32[]{:S(2)}) copy-start(bf16[1,1,1,256,2048]{4,3,2,1,0:T(8,128)(2,1)S(1)} %collective-permute-done) | copy-start | bytes 3145732
  154.3 128.2 %copy-start.5 = (bf16[1,1,1,256,2048]{4,3,2,1,0:T(8,128)(2,1)}, bf16[1,1,1,256,2048]{4,3,2,1,0:T(8,128)(2,1)S(1)}, u32[]{:S(2)}) copy-start(bf16[1,1,1,256,2048]{4,3,2,1,0:T(8,128)(2,1)S(1)} %collective-permute-done.1) | copy-start | bytes 3145732
  156.4 128.1 %collective-permute-start.2 = (bf16[3,1,1,256,2048]{4,3,2,1,0:T(8,128)(2,1)}, bf16[3,1,1,256,2048]{4,3,2,1,0:T(8,128)(2,1)}, u32[]{:S(2)}, u32[]{:S(2)}) collective-permute-start(bf16[3,1,1,256,2048]{4,3,2,1,0:T(8,128)(2,1)} %pad_maximum_fusion.1), channel_id=1, source_target_pairs={{0,1},{1,2},{2,3},{3,4},{4,5},{5,6},{6,7},{7,8},{8,9},{9,10},{10,1... | collective-permute-start | bytes 9437192 | tf_op jit(solution)/shard_map/ppermute | solution.py:38
  161.3 123.1 %collective-permute-start.3 = (bf16[3,1,1,256,2048]{4,3,2,1,0:T(8,128)(2,1)}, bf16[3,1,1,256,2048]{4,3,2,1,0:T(8,128)(2,1)}, u32[]{:S(2)}, u32[]{:S(2)}) collective-permute-start(bf16[3,1,1,256,2048]{4,3,2,1,0:T(8,128)(2,1)} %pad_maximum_fusion.1), channel_id=1, source_target_pairs={{1,0},{2,1},{3,2},{4,3},{5,4},{6,5},{7,6},{8,7},{9,8},{10,9},{11,1... | collective-permute-start | bytes 9437192 | tf_op jit(solution)/shard_map/ppermute | solution.py:39
  293.9 86.6 %copy-start.3 = (bf16[1,1,1,256,1024]{4,3,2,1,0:T(8,128)(2,1)S(1)}, bf16[1,1,1,256,1024]{4,3,2,1,0:T(8,128)(2,1)}, u32[]{:S(2)}) copy-start(bf16[1,1,1,256,1024]{4,3,2,1,0:T(8,128)(2,1)} %param.7) | copy-start | bytes 1572868
  298.4 2.2 copy-start
  309.2 2.2 copy-start
  320.0 2.2 copy-start
  330.8 2.2 copy-start
  341.6 2.2 copy-start
  352.4 2.2 copy-start
  363.3 2.2 copy-start
  374.1 2.2 copy-start
Sparse Core Ops, SparseCore 0:
  139.9 138.5 all-gather.2
